TPU v7x, 128 devices: a whole 4x4x4 slice. The times are simulated.
128 devices in a mesh: section: 2 (over core), seq: 4 (over x), dp: 16 (over z, y).
Axes of the slice: x: 4, y: 4, z: 4, core: 2. Of those that a mesh axis runs over, the one named last changes fastest.
Arguments:
- section_input: bfloat16 [2, 16, 512, 4096], P('section', 'dp', 'seq'), may hold values from -6 to 6
- saved_qkv: bfloat16 [2, 16, 512, 3, 2048], P('section', 'dp', None, None, 'seq'), may hold values from -14 to 14
- modulation: float32 [2, 16, 2, 4096], P('section', 'dp'), may hold values from -4 to 4
- w_qkv: bfloat16 [2, 4096, 3, 2048], P('section', 'dp', None, 'seq'), may hold values from -0.09375 to 0.09375
- w_out: bfloat16 [2, 2048, 4096], P('section', 'seq'), may hold values from -0.125 to 0.125
- lengths: int32 [16], P('dp'), may hold values from 1 to 512, 5120 in all
- student_out: bfloat16 [16, 512, 4096], P('dp', 'seq'), may hold values from -6 to 6
- teacher_target: bfloat16 [16, 512, 4096], P('dp', 'seq'), may hold values from -6 to 6
Outputs:
- grad_input: bfloat16 [2, 16, 512, 4096], P('section', 'dp', 'seq')
- grad_out: bfloat16 [2, 2048, 4096], P('section', 'seq', 'dp')
Inputs may be any that keep to these rules, and one draw needn't show every extreme that they name: `lengths`: at least one micro-batch is 512 tokens long.
All inputs are finite; a program needn't handle non-finite values. No bound on the sum of `lengths` on one device may be relied on, other than what follows from the above.
Results may differ from a plain program's by a relative error of at most 0.014.
Values may be sent and summed in bfloat16 or wider, within the bound.
A program may use at most 192 MiB of HBM per device.

v0:
```python
import math

import jax
import jax.numpy as jnp
from jax import lax
from jax.sharding import PartitionSpec as P

HEAD_DIM = 128


def in_blocks(value, dim, count):
    dims = value.shape
    tiles = value.reshape(*dims[:dim], count, dims[dim] // count, *dims[dim + 1 :])
    return jnp.moveaxis(tiles, dim, 0)


def sum_at_owner(value, axis, dim):
    count = lax.axis_size(axis)
    tiles = lax.all_to_all(in_blocks(value, dim, count), axis, 0, 0, tiled=True)
    return jnp.sum(tiles, axis=0)


def shifted(value, axis, steps):
    count = lax.axis_size(axis)
    initial, last = (max(0, -steps), min(count, count - steps))
    return lax.ppermute(value, axis, [(source, source + steps) for source in range(initial, last)])


def widen(tensor):
    return lax.optimization_barrier(tensor).astype(jnp.float32)


def contract_rows(left_side, right_side):
    return lax.dot_general(
        left_side, right_side, (((0,), (0,)), ((), ())), preferred_element_type=jnp.float32
    )


def layer_norm_parts(tokens):
    values = tokens.astype(jnp.float32)
    center = values - jnp.mean(values, axis=-1, keepdims=True)
    variance = jnp.mean(center * center, axis=-1, keepdims=True)
    inverse = lax.rsqrt(variance + 1e-06)
    return (center * inverse, inverse)


def attend_backward(saved_rows, d_attn, live_keys, head_size):
    row_total = saved_rows.shape[0]
    feature_width = saved_rows.shape[2]
    head_count = feature_width // head_size
    queries = saved_rows[:, 0].reshape(row_total, head_count, head_size).astype(jnp.float32)
    key_rows = saved_rows[:, 1].reshape(row_total, head_count, head_size).astype(jnp.float32)
    value_rows = saved_rows[:, 2].reshape(row_total, head_count, head_size).astype(jnp.float32)
    factor = 1.0 / math.sqrt(head_size)
    scores = jnp.einsum("qhd,khd->hqk", queries, key_rows) * factor
    scores = jnp.where(live_keys[None, None, :], scores, -1e30)
    peak_score = jnp.max(scores, axis=-1, keepdims=True)
    weights = jnp.exp(scores - peak_score)
    weights = weights / jnp.sum(weights, axis=-1, keepdims=True)
    rounded = widen(weights.astype(jnp.bfloat16))
    attn_mixed = jnp.einsum("hqk,khd->qhd", rounded, value_rows).astype(jnp.bfloat16)
    upstream = d_attn.reshape(row_total, head_count, head_size).astype(jnp.float32)
    d_weights = jnp.einsum("qhd,khd->hqk", upstream, value_rows)
    delta_rows = jnp.einsum("qhd,qhd->hq", upstream, widen(attn_mixed))
    d_scores = widen((weights * (d_weights - delta_rows[:, :, None]) * factor).astype(jnp.bfloat16))
    grad_q = jnp.einsum("hqk,khd->qhd", d_scores, key_rows).astype(jnp.bfloat16)
    grad_k = jnp.einsum("hqk,qhd->khd", d_scores, queries).astype(jnp.bfloat16)
    grad_v = jnp.einsum("hqk,qhd->khd", rounded, upstream).astype(jnp.bfloat16)
    stacked = jnp.stack([grad_q, grad_k, grad_v], axis=1).reshape(row_total, 3, feature_width)
    return (attn_mixed.reshape(row_total, feature_width), stacked)


def body(section_input, saved_qkv, modulation, w_qkv, w_out, lengths, student_out, teacher_target):
    section_total = lax.axis_size("section")
    section_pos = lax.axis_index("section")
    seq_pos = lax.axis_index("seq")
    micro_count = section_input.shape[1]
    shard_rows = section_input.shape[2]
    model_width = section_input.shape[3]
    capacity = saved_qkv.shape[2]
    local_width = saved_qkv.shape[4]
    inputs = section_input[0]
    saved_all = saved_qkv[0]
    mods = modulation[0]
    weight_rows = lax.all_gather(w_qkv[0], "dp", axis=0, tiled=True)
    weight_flat = weight_rows.reshape(model_width, 3 * local_width)
    weight_out = w_out[0]
    normed_all, inverse_all = layer_norm_parts(inputs)
    positions = seq_pos * shard_rows + jnp.arange(shard_rows, dtype=jnp.int32)
    row_live = positions[None, :] < lengths[:, None]
    gap = student_out.astype(jnp.float32) - teacher_target.astype(jnp.float32)
    loss_grad = jnp.where(row_live[:, :, None], gap, 0.0).astype(jnp.bfloat16)
    key_positions = jnp.arange(capacity, dtype=jnp.int32)

    def attend_live(saved_rows, d_attn, live_keys):
        attn_mixed, d_saved = attend_backward(saved_rows, d_attn, live_keys, HEAD_DIM)
        return (attn_mixed, d_saved.reshape(capacity, 3 * local_width))

    def section_work(d_output, slot_index, is_live):
        mod_rows = lax.dynamic_index_in_dim(mods, slot_index, 0, False)
        scale_term = mod_rows[0]
        gate_term = mod_rows[1]
        d_branch = (gate_term * d_output.astype(jnp.float32)).astype(jnp.bfloat16)
        d_branch = jnp.where(is_live, d_branch, jnp.zeros_like(d_branch))
        branch_full = lax.all_gather(d_branch, "seq", axis=0, tiled=True)
        live_length = lengths[slot_index]
        live_keys = key_positions < live_length
        saved_rows = lax.dynamic_index_in_dim(saved_all, slot_index, 0, False)

        def attend_branch(branch_rows):
            d_attn = jnp.dot(branch_rows, weight_out.T, preferred_element_type=jnp.float32).astype(
                jnp.bfloat16
            )
            return attend_live(saved_rows, d_attn, live_keys)

        def attend_none(branch_rows):
            return (
                jnp.zeros((capacity, local_width), jnp.bfloat16),
                jnp.zeros((capacity, 3 * local_width), jnp.bfloat16),
            )

        attn_mixed, flat_grads = lax.cond(is_live, attend_branch, attend_none, branch_full)
        d_mod = sum_at_owner(
            lax.cond(
                is_live,
                lambda start_row: jnp.dot(
                    flat_grads, weight_flat.T, preferred_element_type=jnp.float32
                ),
                lambda start_row: jnp.zeros(
                    (shard_rows * lax.axis_size("seq"), model_width), jnp.float32
                ),
                jnp.int32(0),
            ),
            "seq",
            0,
        )
        normed = lax.dynamic_index_in_dim(normed_all, slot_index, 0, False)
        inverse = lax.dynamic_index_in_dim(inverse_all, slot_index, 0, False)
        d_norm = d_mod * (1.0 + scale_term)
        d_layer = inverse * (
            d_norm
            - jnp.mean(d_norm, axis=-1, keepdims=True)
            - normed * jnp.mean(d_norm * normed, axis=-1, keepdims=True)
        )
        d_input = (d_output.astype(jnp.float32) + d_layer).astype(jnp.bfloat16)
        d_input = jnp.where(is_live, d_input, jnp.zeros_like(d_input))
        return (d_input, attn_mixed, branch_full)

    def put_slot(store, fresh, slot_index, is_live):
        older = lax.dynamic_index_in_dim(store, slot_index, 0, False)
        return lax.dynamic_update_index_in_dim(
            store, jnp.where(is_live, fresh, older), slot_index, 0
        )

    def tick(tick_num, carry):
        incoming, grads_in, mixed_store, branch_store = carry
        slot_raw = tick_num - (section_total - 1 - section_pos)
        is_live = jnp.logical_and(slot_raw >= 0, slot_raw < micro_count)
        slot_index = jnp.clip(slot_raw, 0, micro_count - 1)
        last_grad = lax.dynamic_index_in_dim(loss_grad, slot_index, 0, False)
        d_output = jnp.where(section_pos == section_total - 1, last_grad, incoming)
        d_input, attn_mixed, branch_full = section_work(d_output, slot_index, is_live)
        grads_in = put_slot(grads_in, d_input, slot_index, is_live)
        mixed_store = put_slot(mixed_store, attn_mixed, slot_index, is_live)
        branch_store = put_slot(branch_store, branch_full, slot_index, is_live)
        incoming = shifted(d_input, "section", -1)
        return (incoming, grads_in, mixed_store, branch_store)

    start_carry = (
        jnp.zeros((shard_rows, model_width), jnp.bfloat16),
        jnp.zeros((micro_count, shard_rows, model_width), jnp.bfloat16),
        jnp.zeros((micro_count, capacity, local_width), jnp.bfloat16),
        jnp.zeros((micro_count, capacity, model_width), jnp.bfloat16),
    )
    final_carry = lax.fori_loop(0, section_total + micro_count - 1, tick, start_carry)
    grads_in = final_carry[1]
    mixed_store = final_carry[2]
    branch_store = final_carry[3]
    out_local = contract_rows(
        mixed_store.reshape(micro_count * capacity, local_width),
        branch_store.reshape(micro_count * capacity, model_width),
    )
    out_slice = lax.psum_scatter(out_local, "dp", scatter_dimension=1, tiled=True)
    grad_input = grads_in[None]
    grad_out = out_slice.astype(jnp.bfloat16)[None]
    return (grad_input, grad_out)


def solution(mesh):
    in_specs = (
        P("section", "dp", "seq", None),
        P("section", "dp", None, None, "seq"),
        P("section", "dp", None, None),
        P("section", "dp", None, "seq"),
        P("section", "seq", None),
        P("dp"),
        P("dp", "seq", None),
        P("dp", "seq", None),
    )
    out_specs = (P("section", "dp", "seq", None), P("section", "seq", "dp"))
    return jax.shard_map(body, mesh=mesh, in_specs=in_specs, out_specs=out_specs, check_vma=False)
```

profile of v0, /device:TPU:0, one launch (start us, length us, event | category | flops | bytes accessed | tf_op | source)
XLA Modules:
  0.0 575.2 jit_solution(12609359654335451927)
XLA Ops:
  10.3 2.7 copy.32
  13.6 3.3 fusion.29
  17.0 96.1 %all-gather.4.cloned.1.call-done = bf16[1,4096,3,512]{1,3,2,0:T(8,128)(2,1)} async-done(((bf16[1,256,3,512]{1,3,2,0:T(8,128)(2,1)}), bf16[1,4096,3,512]{1,3,2,0:T(8,128)(2,1)}) %all-gather.4.cloned.1.call-update) | async-done | bytes 12582928 | tf_op jit(solution)/shard_map/all_gather | solution.py:85
  113.0 16.6 %copy.34 = bf16[4096,1536]{1,0:T(8,128)(2,1)} copy(bf16[4096,1536]{0,1:T(8,128)(2,1)} %bitcast.151) | data formatting | bytes 25165824
  131.7 2.6 broadcast_in_dim.89
  134.2 339.5 %while.22 = (s32[]{:T(128)}, bf16[128,4096]{1,0:T(8,128)(2,1)S(1)}, bf16[1,128,4096]{2,1,0:T(8,128)(2,1)}, bf16[1,512,512]{1,2,0:T(8,128)(2,1)}, bf16[1,512,4096...) while((s32[]{:T(128)}, bf16[128,4096]{1,0:T(8,128)(2,1)S(1)}, ...), condition=%wide.region_12.13_spmd.clone, body=%wide.region_2.12_spmd.clone.sunk | while | flops 10230434816 | bytes 286427392 | solution.py:175
  135.8 48.5 %all-gather.6.cloned.1.call-done = bf16[512,4096]{1,0:T(8,128)(2,1)} async-done(((bf16[128,4096]{1,0:T(8,128)(2,1)}), bf16[512,4096]{1,0:T(8,128)(2,1)}) %all-gather.6.cloned.1.call-update) | async-done | bytes 4194320 | tf_op jit(solution)/shard_map/while/body/eval_jaxpr/all_gather | solution.py:105
  185.6 4.3 conditional.7
  185.6 4.3 broadcast.153
  189.9 5.8 %all-to-all-start = ((f32[4,128,4096]{2,1,0:T(8,128)}), f32[4,128,4096]{2,1,0:T(8,128)}, u32[]{:S(2)}, u32[]{:S(2)}) async-start(f32[4,128,4096]{2,1,0:T(8,128)} %bitcast.137), calls=%async_computation | async-start | bytes 16777216 | tf_op jit(solution)/shard_map/while/body/eval_jaxpr/all_to_all | solution.py:19
  196.6 71.3 %all-to-all-done = f32[4,128,4096]{2,1,0:T(8,128)} async-done(((f32[4,128,4096]{2,1,0:T(8,128)}), f32[4,128,4096]{2,1,0:T(8,128)}, u32[]{:S(2)}, u32[]{:S(2)}) %all-to-all-start) | async-done | bytes 8388640 | tf_op jit(solution)/shard_map/while/body/eval_jaxpr/all_to_all | solution.py:19
  267.9 4.2 reduce_sum.85
  279.9 22.3 %collective-permute-done = bf16[128,4096]{1,0:T(8,128)(2,1)S(1)} collective-permute-done((bf16[128,4096]{1,0:T(8,128)(2,1)S(1)}, bf16[128,4096]{1,0:T(8,128)(2,1)S(1)}, u32[]{:S(2)}, u32[]{:S(2)}) %collective-permute-start) | collective-permute-done | bytes 1048608 | tf_op jit(solution)/shard_map/while/body/eval_jaxpr/ppermute | solution.py:26
  303.7 50.5 %all-gather.6.cloned.1.call-done = bf16[512,4096]{1,0:T(8,128)(2,1)} async-done(((bf16[128,4096]{1,0:T(8,128)(2,1)}), bf16[512,4096]{1,0:T(8,128)(2,1)}) %all-gather.6.cloned.1.call-update) | async-done | bytes 4194320 | tf_op jit(solution)/shard_map/while/body/eval_jaxpr/all_gather | solution.py:105
  354.2 17.4 %conditional.6 = (bf16[512,512]{0,1:T(8,128)(2,1)S(1)}, bf16[512,1536]{0,1:T(8,128)(2,1)}) conditional(s32[]{:T(128)} %convert_element_type.172, () %tuple.86, (s32[1]{0:T(128)}, s32[512]{0:T(512)S(1)}, bf16[1,512,3,512]{1,3,2,0:T(8,128)(2,1)}, bf16[512,4096]{1,0:T(8,128)(2,1)}, bf16[512,4096]{1,0:T(8,128)(2,1)}) %tuple.87), branch_computations={%region_3.3_spmd, %region_4.6_spmd} | conditional | flops 3773561856 | bytes 101756056 | solution.py:122
  356.3 3.6 fusion.36
  360.0 2.9 fusion.7
  371.6 12.2 %conditional.7 = (f32[512,4096]{1,0:T(8,128)}) conditional(s32[]{:T(128)} %convert_element_type.172, () %tuple.85, (bf16[512,1536]{0,1:T(8,128)(2,1)}, bf16[4096,1536]{1,0:T(8,128)(2,1)}) %tuple.88), branch_computations={%region_7.7_spmd, %region_8.8_spmd} | conditional | flops 6442450944 | bytes 22544392 | solution.py:124
  371.6 12.2 %fusion.37 = f32[512,4096]{1,0:T(8,128)} fusion(bf16[512,1536]{0,1:T(8,128)(2,1)} %get-tuple-element.422, bf16[4096,1536]{1,0:T(8,128)(2,1)} %get-tuple-element.358), kind=kOutput, calls=%fused_computation.65 | convolution fusion | flops 6442450944 | bytes 22544384 | tf_op jit(solution)/shard_map/while/body/eval_jaxpr/cond/branch_1_fun/dot_general | solution.py:126
  383.8 5.8 %all-to-all-start = ((f32[4,128,4096]{2,1,0:T(8,128)}), f32[4,128,4096]{2,1,0:T(8,128)}, u32[]{:S(2)}, u32[]{:S(2)}) async-start(f32[4,128,4096]{2,1,0:T(8,128)} %bitcast.137), calls=%async_computation | async-start | bytes 16777216 | tf_op jit(solution)/shard_map/while/body/eval_jaxpr/all_to_all | solution.py:19
  390.6 69.1 %all-to-all-done = f32[4,128,4096]{2,1,0:T(8,128)} async-done(((f32[4,128,4096]{2,1,0:T(8,128)}), f32[4,128,4096]{2,1,0:T(8,128)}, u32[]{:S(2)}, u32[]{:S(2)}) %all-to-all-start) | async-done | bytes 8388640 | tf_op jit(solution)/shard_map/while/body/eval_jaxpr/all_to_all | solution.py:19
  459.7 4.2 reduce_sum.85
  473.7 7.9 %fusion.26 = f32[512,4096]{1,0:T(8,128)} fusion(bf16[1,512,4096]{2,1,0:T(8,128)(2,1)} %get-tuple-element.385, bf16[1,512,512]{1,2,0:T(8,128)(2,1)} %get-tuple-element.384), kind=kOutput, calls=%fused_computation.48 | convolution fusion | flops 2147483648 | bytes 13107200 | tf_op jit(solution)/shard_map/dot_general | solution.py:34
  481.7 85.2 %reduce-scatter.2.cloned.1.call-done = f32[512,256]{1,0:T(8,128)} async-done(((f32[512,4096]{1,0:T(8,128)}), f32[512,256]{1,0:T(8,128)}) %reduce-scatter.2.cloned.1.call-update) | async-done | bytes 524304 | tf_op jit(solution)/shard_map/reduce_scatter | solution.py:183
  (101 shorter events, 42.4 us)
Async XLA Ops:
  7.2 105.9 %all-gather.4.cloned.1.call-start = ((), (), s32[]{:S(2)}) async-start(), calls=%async_computation.3 | async-start | bytes 13369344 | tf_op jit(solution)/shard_map/all_gather | solution.py:85
  9.5 3.5 copy-start.13
  10.3 3.4 copy-start.14
  131.7 2.6 copy-start.15
  134.2 50.0 %all-gather.6.cloned.1.call-start = ((), (), s32[]{:S(2)}) async-start(), calls=%async_computation.4 | async-start | bytes 5242880 | tf_op jit(solution)/shard_map/while/body/eval_jaxpr/all_gather | solution.py:105
  189.9 5.8 %copy-start.11 = (bf16[1,512,512]{1,2,0:T(8,128)(2,1)S(1)}, bf16[1,512,512]{1,2,0:T(8,128)(2,1)}, u32[]{:S(2)}) copy-start(bf16[1,512,512]{1,2,0:T(8,128)(2,1)} %get-tuple-element.624) | copy-start | bytes 1572868 | tf_op jit(solution)/shard_map/while
  189.9 78.1 %all-to-all-start = ((f32[4,128,4096]{2,1,0:T(8,128)}), f32[4,128,4096]{2,1,0:T(8,128)}, u32[]{:S(2)}, u32[]{:S(2)}) async-start(f32[4,128,4096]{2,1,0:T(8,128)} %bitcast.137), calls=%async_computation | async-start | bytes 16777216 | tf_op jit(solution)/shard_map/while/body/eval_jaxpr/all_to_all | solution.py:19
  272.1 2.5 copy-start.9
  274.6 4.0 copy-start.1
  274.6 4.2 copy-start.4
  277.1 2.7 copy-start.10
  277.1 25.1 %collective-permute-start = (bf16[128,4096]{1,0:T(8,128)(2,1)S(1)}, bf16[128,4096]{1,0:T(8,128)(2,1)S(1)}, u32[]{:S(2)}, u32[]{:S(2)}) collective-permute-start(bf16[128,4096]{1,0:T(8,128)(2,1)S(1)} %get-tuple-element.596), channel_id=1, source_target_pairs={{64,0},{65,1},{66,2},{67,3},{68,4},{69,5},{70,6},{71,7},{72,8},{73... | collective-permute-start | bytes 3145736 | tf_op jit(solution)/shard_map/while/body/eval_jaxpr/ppermute | solution.py:26
  279.9 22.3 %copy-start.2 = (bf16[1,512,4096]{2,1,0:T(8,128)(2,1)}, bf16[1,512,4096]{2,1,0:T(8,128)(2,1)S(1)}, u32[]{:S(2)}) copy-start(bf16[1,512,4096]{2,1,0:T(8,128)(2,1)S(1)} %fusion.63) | copy-start | bytes 12582916 | tf_op jit(solution)/shard_map/while
  302.2 52.0 %all-gather.6.cloned.1.call-start = ((), (), s32[]{:S(2)}) async-start(), calls=%async_computation.4 | async-start | bytes 5242880 | tf_op jit(solution)/shard_map/while/body/eval_jaxpr/all_gather | solution.py:105
  360.0 3.4 copy-start.5
  360.0 4.9 copy-start.16
  363.4 3.9 copy-start.7
  383.8 5.8 %copy-start.11 = (bf16[1,512,512]{1,2,0:T(8,128)(2,1)S(1)}, bf16[1,512,512]{1,2,0:T(8,128)(2,1)}, u32[]{:S(2)}) copy-start(bf16[1,512,512]{1,2,0:T(8,128)(2,1)} %get-tuple-element.624) | copy-start | bytes 1572868 | tf_op jit(solution)/shard_map/while
  383.8 75.9 %all-to-all-start = ((f32[4,128,4096]{2,1,0:T(8,128)}), f32[4,128,4096]{2,1,0:T(8,128)}, u32[]{:S(2)}, u32[]{:S(2)}) async-start(f32[4,128,4096]{2,1,0:T(8,128)} %bitcast.137), calls=%async_computation | async-start | bytes 16777216 | tf_op jit(solution)/shard_map/while/body/eval_jaxpr/all_to_all | solution.py:19
  466.4 4.0 copy-start.1
  466.4 4.2 copy-start.4
  468.9 2.7 copy-start.10
  468.9 4.7 collective-permute-start
  473.7 93.2 %reduce-scatter.2.cloned.1.call-start = ((), (), s32[]{:S(2)}) async-start(), calls=%async_computation.2 | async-start | bytes 8912896 | tf_op jit(solution)/shard_map/reduce_scatter | solution.py:183
  (10 other events, 17.3 us)
Sparse Core Ops, SparseCore 0:
  10.7 102.2 all-gather.3
  136.7 47.4 all-gather.5
  304.7 49.4 all-gather.5
  481.8 85.0 reduce-scatter.1
where the time goes:
time: 576 us; the launch traced here: 575 us
  waiting for transfers between devices  445 us (77%)
  local copies, waits for them, and re-layouts  37.6 us (7%)
  other arithmetic  33.7 us (6%)
  matrix products  29.5 us (5%)
  starting transfers between devices  14.5 us (3%)
  between operations  14.5 us (3%)
    all_to_all x2, waiting for transfers between devices, sum_at_owner(): tiles = lax.all_to_all(in_blocks(value, dim, count), axis, 0, 0, tiled=True)  140 us
    all_gather x2, waiting for transfers between devices, section_work(): branch_full = lax.all_gather(d_branch, 'seq', axis=0, tiled=True)  99 us
    all_gather x1, waiting for transfers between devices, body(): weight_rows = lax.all_gather(w_qkv[0], 'dp', axis=0, tiled=True)  96.1 us
    reduce_scatter x1, waiting for transfers between devices, body(): lax.psum_scatter(out_local, 'dp', scatter_dimension=1, tiled=True)  85.2 us
    ppermute x2, waiting for transfers between devices, shifted(): lax.ppermute(value, axis, [(source, source + steps) for source in range(i...  24.3 us
    unnamed x9, local copies, waits for them, and re-layouts  21.6 us
    dot_general x1, matrix products, section_work(): jnp.dot(flat_grads, weight_flat.T, preferred_element_type=jnp.float32)  12.2 us
    all_to_all x2, starting transfers between devices, sum_at_owner(): tiles = lax.all_to_all(in_blocks(value, dim, count), axis, 0, 0, tiled=True)  11.6 us
  transfers between devices with their start and end apart: 8, of which 8 were waited for; matrix products, arithmetic and copies ran while one was open for 2% of the time, Pallas kernels for 0%

commit v1 on v0

v1 whole, which is shorter than its diff:
```python
import math

import jax
import jax.numpy as jnp
from jax import lax
from jax.sharding import PartitionSpec as P

HEAD_DIM = 128


def widen(tensor):
    return lax.optimization_barrier(tensor).astype(jnp.float32)


def layer_norm_parts(tokens):
    values = tokens.astype(jnp.float32)
    center = values - jnp.mean(values, axis=-1, keepdims=True)
    variance = jnp.mean(center * center, axis=-1, keepdims=True)
    inverse = lax.rsqrt(variance + 1e-06)
    return (center * inverse, inverse)


def attend_forward(saved_rows, live_keys, head_size):
    row_total = saved_rows.shape[0]
    feature_width = saved_rows.shape[2]
    head_count = feature_width // head_size
    queries = saved_rows[:, 0].reshape(row_total, head_count, head_size).astype(jnp.float32)
    key_rows = saved_rows[:, 1].reshape(row_total, head_count, head_size).astype(jnp.float32)
    value_rows = saved_rows[:, 2].reshape(row_total, head_count, head_size).astype(jnp.float32)
    factor = 1.0 / math.sqrt(head_size)
    scores = jnp.einsum("qhd,khd->hqk", queries, key_rows) * factor
    scores = jnp.where(live_keys[None, None, :], scores, -1e30)
    peak_score = jnp.max(scores, axis=-1, keepdims=True)
    weights = jnp.exp(scores - peak_score)
    weights = weights / jnp.sum(weights, axis=-1, keepdims=True)
    rounded = widen(weights.astype(jnp.bfloat16))
    attn_mixed = jnp.einsum("hqk,khd->qhd", rounded, value_rows).astype(jnp.bfloat16)
    return weights, rounded, attn_mixed


def attend_backward(saved_rows, fwd, d_attn, head_size):
    weights, rounded, attn_mixed = fwd
    row_total = saved_rows.shape[0]
    feature_width = saved_rows.shape[2]
    head_count = feature_width // head_size
    queries = saved_rows[:, 0].reshape(row_total, head_count, head_size).astype(jnp.float32)
    key_rows = saved_rows[:, 1].reshape(row_total, head_count, head_size).astype(jnp.float32)
    value_rows = saved_rows[:, 2].reshape(row_total, head_count, head_size).astype(jnp.float32)
    factor = 1.0 / math.sqrt(head_size)
    upstream = d_attn.reshape(row_total, head_count, head_size).astype(jnp.float32)
    d_weights = jnp.einsum("qhd,khd->hqk", upstream, value_rows)
    delta_rows = jnp.einsum("qhd,qhd->hq", upstream, widen(attn_mixed))
    d_scores = widen((weights * (d_weights - delta_rows[:, :, None]) * factor).astype(jnp.bfloat16))
    grad_q = jnp.einsum("hqk,khd->qhd", d_scores, key_rows).astype(jnp.bfloat16)
    grad_k = jnp.einsum("hqk,qhd->khd", d_scores, queries).astype(jnp.bfloat16)
    grad_v = jnp.einsum("hqk,qhd->khd", rounded, upstream).astype(jnp.bfloat16)
    stacked = jnp.stack([grad_q, grad_k, grad_v], axis=1).reshape(row_total, 3 * feature_width)
    return stacked


def body(section_input, saved_qkv, modulation, w_qkv, w_out, lengths, student_out, teacher_target):
    section_total = lax.axis_size("section")
    section_pos = lax.axis_index("section")
    seq_pos = lax.axis_index("seq")
    inputs = section_input[0, 0]
    saved_rows = saved_qkv[0, 0]
    mods = modulation[0, 0]
    weight_out = w_out[0]
    shard_rows, model_width = inputs.shape
    capacity = saved_rows.shape[0]
    local_width = saved_rows.shape[2]
    live_length = lengths[0]

    weight_flat = lax.all_gather(w_qkv[0], "dp", axis=0, tiled=True).reshape(
        model_width, 3 * local_width
    )
    normed, inverse = layer_norm_parts(inputs)
    positions = seq_pos * shard_rows + jnp.arange(shard_rows, dtype=jnp.int32)
    row_live = positions < live_length
    gap = student_out[0].astype(jnp.float32) - teacher_target[0].astype(jnp.float32)
    loss_grad = jnp.where(row_live[:, None], gap, 0.0).astype(jnp.bfloat16)
    live_keys = jnp.arange(capacity, dtype=jnp.int32) < live_length
    fwd = attend_forward(saved_rows, live_keys, HEAD_DIM)
    attn_mixed = fwd[2].reshape(capacity, local_width)
    scale_term = mods[0]
    gate_term = mods[1]

    def section_work(d_output):
        d_branch = (gate_term * d_output.astype(jnp.float32)).astype(jnp.bfloat16)
        branch_full = lax.all_gather(d_branch, "seq", axis=0, tiled=True)
        out_local = jnp.dot(attn_mixed.T, branch_full, preferred_element_type=jnp.float32)
        d_attn = jnp.dot(branch_full, weight_out.T, preferred_element_type=jnp.float32).astype(
            jnp.bfloat16
        )
        flat_grads = attend_backward(saved_rows, fwd, d_attn, HEAD_DIM)
        d_mod_part = jnp.dot(flat_grads, weight_flat.T, preferred_element_type=jnp.float32)
        d_mod = lax.psum_scatter(
            d_mod_part.astype(jnp.bfloat16), "seq", scatter_dimension=0, tiled=True
        ).astype(jnp.float32)
        d_norm = d_mod * (1.0 + scale_term)
        d_layer = inverse * (
            d_norm
            - jnp.mean(d_norm, axis=-1, keepdims=True)
            - normed * jnp.mean(d_norm * normed, axis=-1, keepdims=True)
        )
        d_input = (d_output.astype(jnp.float32) + d_layer).astype(jnp.bfloat16)
        return d_input, out_local

    incoming = loss_grad
    grad_input = None
    out_local = None
    for stage in reversed(range(section_total)):
        d_input, stage_out = section_work(incoming)
        here = section_pos == stage
        grad_input = d_input if grad_input is None else jnp.where(here, d_input, grad_input)
        out_local = stage_out if out_local is None else jnp.where(here, stage_out, out_local)
        if stage > 0:
            incoming = lax.ppermute(d_input, "section", [(stage, stage - 1)])
    out_slice = lax.psum_scatter(out_local, "dp", scatter_dimension=1, tiled=True)
    return (grad_input[None, None], out_slice.astype(jnp.bfloat16)[None])


def solution(mesh):
    in_specs = (
        P("section", "dp", "seq", None),
        P("section", "dp", None, None, "seq"),
        P("section", "dp", None, None),
        P("section", "dp", None, "seq"),
        P("section", "seq", None),
        P("dp"),
        P("dp", "seq", None),
        P("dp", "seq", None),
    )
    out_specs = (P("section", "dp", "seq", None), P("section", "seq", "dp"))
    return jax.shard_map(body, mesh=mesh, in_specs=in_specs, out_specs=out_specs, check_vma=False)
```

time: 576 us -> 449 us (0.78)
  waiting for transfers between devices: 445 us -> 347 us
  local copies, waits for them, and re-layouts: 37.6 us -> 11.4 us
  matrix products: 29.5 us -> 52.9 us
  other arithmetic: 33.7 us -> 20.5 us
  starting transfers between devices: 14.5 us -> 1.93 us
    all_to_all x2 -> x0, waiting for transfers between devices: 140 us -> none  [sum_at_owner(): tiles = lax.all_to_all(in_blocks(value, dim, count), axis, 0, 0, tiled=True)]
    reduce_scatter x0 -> x2, waiting for transfers between devices: none -> 79.9 us  [section_work(): lax.psum_scatter(d_mod_part.astype(jnp.bfloat16), 'seq', scatter_dimensio...]
    ppermute x2 -> x1, waiting for transfers between devices: 24.3 us -> 3.25 us  [body(): incoming = lax.ppermute(d_input, 'section', [(stage, stage - 1)])]
    dot_general x3 -> x5, matrix products: 10.7 us -> 23 us  [the longest x2 12 us: section_work(): jnp.dot(branch_full, weight_out.T, preferred_element_type=jnp.float32)]
    all_to_all x2 -> x0, starting transfers between devices: 11.6 us -> none  [sum_at_owner(): tiles = lax.all_to_all(in_blocks(value, dim, count), axis, 0, 0, tiled=True)]
    unnamed x9 -> x52, local copies, waits for them, and re-layouts: 21.6 us -> 10.5 us
    all_gather x2, waiting for transfers between devices: 99 us -> 88 us  [section_work(): branch_full = lax.all_gather(d_branch, 'seq', axis=0, tiled=True)]
    reduce_sum x2 -> x0, other arithmetic: 8.37 us -> none  [sum_at_owner(): return jnp.sum(tiles, axis=0)]
  transfers between devices with their start and end apart: 8 -> 7, of which waited for: 8 -> 7; matrix products, arithmetic and copies ran while one was open for 2% -> 8% of each run, Pallas kernels for 0% -> 0%
where the time goes in v1:
time: 449 us; the launch traced here: 448 us
  waiting for transfers between devices  347 us (77%)
  matrix products  52.9 us (12%)
  other arithmetic  20.5 us (5%)
  between operations  15.1 us (3%)
  local copies, waits for them, and re-layouts  11.4 us (3%)
    all_gather x1, waiting for transfers between devices, body(): lax.all_gather(w_qkv[0], 'dp', axis=0, tiled=True)  91.1 us
    all_gather x2, waiting for transfers between devices, section_work(): branch_full = lax.all_gather(d_branch, 'seq', axis=0, tiled=True)  88 us
    reduce_scatter x1, waiting for transfers between devices, body(): lax.psum_scatter(out_local, 'dp', scatter_dimension=1, tiled=True)  84.2 us
    reduce_scatter x2, waiting for transfers between devices, section_work(): lax.psum_scatter(d_mod_part.astype(jnp.bfloat16), 'seq', scatter_dimensio...  79.9 us
    dot_general x2, matrix products, section_work(): jnp.dot(flat_grads, weight_flat.T, preferred_element_type=jnp.float32)  20.3 us
    dot_general x2, matrix products, section_work(): jnp.dot(branch_full, weight_out.T, preferred_element_type=jnp.float32)  12 us
    dot_general x2, matrix products, section_work(): jnp.dot(attn_mixed.T, branch_full, preferred_element_type=jnp.float32)  10.6 us
    unnamed x52, local copies, waits for them, and re-layouts  10.5 us
  transfers between devices with their start and end apart: 7, of which 7 were waited for; matrix products, arithmetic and copies ran while one was open for 8% of the time, Pallas kernels for 0%

profile of v1, /device:TPU:0, one launch (start us, length us, event | category | flops | bytes accessed | tf_op | source)
XLA Modules:
  0.0 448.5 jit_solution(951202817322332470)
XLA Ops:
  8.8 3.0 fusion.6
  13.1 1.7 copy.26
  15.7 3.6 fusion.52
  19.4 2.8 fusion.50
  22.7 39.9 %all-gather.5.cloned.1.call-done = bf16[512,4096]{1,0:T(8,128)(2,1)} async-done(((bf16[128,4096]{1,0:T(8,128)(2,1)}), bf16[512,4096]{1,0:T(8,128)(2,1)}) %all-gather.5.cloned.1.call-update) | async-done | bytes 4194320 | tf_op jit(solution)/shard_map/all_gather | solution.py:90
  62.6 6.0 %fusion.42 = (f32[4,512]{1,0:T(4,128)S(1)}, bf16[512,512]{0,1:T(8,128)(2,1)S(1)}) fusion(bf16[512,4,128]{0,2,1:T(8,128)(2,1)S(1)} %bitcast.149, bf16[512,4096]{1,0:T(8,128)(2,1)} %all-gather.5.cloned.1.call-done, bf16[1,512,4096]{2,1,0:T(8,128)(2,1)} %param.12), kind=kOutput, calls=%fused_computation.66 | convolution fusion | flops 2148792320 | bytes 9445376 | tf_op jit(solution)/shard_map/dot_general | solution.py:92
  72.5 1.4 pad_maximum_fusion
  73.8 91.1 %all-gather.9.cloned.1.call-done = bf16[1,4096,3,512]{1,3,2,0:T(8,128)(2,1)} async-done(((bf16[1,256,3,512]{1,3,2,0:T(8,128)(2,1)}), bf16[1,4096,3,512]{1,3,2,0:T(8,128)(2,1)}) %all-gather.9.cloned.1.call-update) | async-done | bytes 12582928 | tf_op jit(solution)/shard_map/all_gather | solution.py:74
  165.0 11.6 %convolution_convert_fusion.1 = bf16[512,4096]{1,0:T(8,128)(2,1)} fusion(bf16[512,1536]{0,1:T(8,128)(2,1)} %bitcast.162, bf16[4096,1536]{0,1:T(8,128)(2,1)} %bitcast.174), kind=kOutput, calls=%fused_computation.3 | convolution fusion | flops 6444548096 | bytes 18350080 | tf_op jit(solution)/shard_map/dot_general | solution.py:96
  178.5 44.3 %reduce-scatter.4.cloned.1.call-done = bf16[128,4096]{1,0:T(8,128)(2,1)} async-done(((bf16[512,4096]{1,0:T(8,128)(2,1)}), bf16[128,4096]{1,0:T(8,128)(2,1)}) %reduce-scatter.4.cloned.1.call-update) | async-done | bytes 1048592 | tf_op jit(solution)/shard_map/reduce_scatter | solution.py:97
  222.8 2.0 fusion.26
  224.8 2.4 fusion.7
  229.5 3.3 collective-permute-done
  235.1 48.1 %all-gather.7.cloned.1.call-done = bf16[512,4096]{1,0:T(8,128)(2,1)} async-done(((bf16[128,4096]{1,0:T(8,128)(2,1)}), bf16[512,4096]{1,0:T(8,128)(2,1)}) %all-gather.7.cloned.1.call-update) | async-done | bytes 4194320 | tf_op jit(solution)/shard_map/all_gather | solution.py:90
  283.2 6.0 %fusion.43 = (f32[4,512]{1,0:T(4,128)S(1)}, bf16[512,512]{0,1:T(8,128)(2,1)S(1)}) fusion(bf16[512,4,128]{0,2,1:T(8,128)(2,1)} %bitcast.150, bf16[512,4096]{1,0:T(8,128)(2,1)} %all-gather.7.cloned.1.call-done, bf16[1,512,4096]{2,1,0:T(8,128)(2,1)} %param.12), kind=kOutput, calls=%fused_computation.67 | convolution fusion | flops 2148792320 | bytes 9445376 | tf_op jit(solution)/shard_map/dot_general | solution.py:92
  294.1 1.4 slice-done.2
  295.5 8.7 %convolution_convert_fusion = bf16[512,4096]{1,0:T(8,128)(2,1)} fusion(bf16[512,1536]{0,1:T(8,128)(2,1)S(1)} %bitcast.163, bf16[4096,1536]{0,1:T(8,128)(2,1)S(1)} %bitcast.177), kind=kOutput, calls=%fused_computation.2 | convolution fusion | flops 6444548096 | bytes 18350080 | tf_op jit(solution)/shard_map/dot_general | solution.py:96
  305.2 4.7 %fusion.53 = f32[512,4096]{1,0:T(8,128)S(1)} fusion(bf16[512,512]{0,1:T(8,128)(2,1)S(1)} %bitcast.151, bf16[512,4096]{1,0:T(8,128)(2,1)} %all-gather.5.cloned.1.call-done), kind=kOutput, calls=%fused_computation.86 | convolution fusion | flops 2147483648 | bytes 13107200 | tf_op jit(solution)/shard_map/dot_general | solution.py:91
  309.9 5.9 %convolution_select_fusion = f32[512,4096]{1,0:T(8,128)} fusion(f32[512,4096]{1,0:T(8,128)S(1)} %fusion.53, bf16[512,512]{0,1:T(8,128)(2,1)S(1)} %bitcast.152, bf16[512,4096]{1,0:T(8,128)(2,1)S(1)} %copy-done.18, pred[]{:T(512)S(6)} %eq.3), kind=kOutput, calls=%fused_computation.1 | convolution fusion | flops 2149580800 | bytes 21495808 | tf_op jit(solution)/shard_map/dot_general | solution.py:91
  315.8 35.6 %reduce-scatter.6.cloned.1.call-done = bf16[128,4096]{1,0:T(8,128)(2,1)} async-done(((bf16[512,4096]{1,0:T(8,128)(2,1)}), bf16[128,4096]{1,0:T(8,128)(2,1)}) %reduce-scatter.6.cloned.1.call-update) | async-done | bytes 1048592 | tf_op jit(solution)/shard_map/reduce_scatter | solution.py:97
  351.5 2.0 fusion.25
  353.5 2.1 fusion.45
  355.6 84.2 %reduce-scatter.8.cloned.1.call-done = f32[512,256]{1,0:T(8,128)} async-done(((f32[512,4096]{1,0:T(8,128)}), f32[512,256]{1,0:T(8,128)}) %reduce-scatter.8.cloned.1.call-update) | async-done | bytes 524304 | tf_op jit(solution)/shard_map/reduce_scatter | solution.py:119
  439.8 1.8 convert_bitcast_fusion.1
  (86 shorter events, 19.7 us)
Async XLA Ops:
  7.2 55.5 %all-gather.5.cloned.1.call-start = ((), (), s32[]{:S(2)}) async-start(), calls=%async_computation.3 | async-start | bytes 5242880 | tf_op jit(solution)/shard_map/all_gather | solution.py:90
  8.7 3.1 copy-start.21
  11.8 153.2 %all-gather.9.cloned.1.call-start = ((), (), s32[]{:S(2)}) async-start(), calls=%async_computation.8 | async-start | bytes 13369344 | tf_op jit(solution)/shard_map/all_gather | solution.py:74
  13.0 209.7 %reduce-scatter.4.cloned.1.call-start = ((), (), s32[]{:S(2)}) async-start(), calls=%async_computation.4 | async-start | bytes 5242880 | tf_op jit(solution)/shard_map/reduce_scatter | solution.py:97
  15.7 3.7 copy-start.3
  15.7 3.7 copy-start.6
  19.4 2.9 copy-start.19
  22.7 45.9 %copy-start.1 = (bf16[4,512,128]{1,2,0:T(8,128)(2,1)}, bf16[4,512,128]{1,2,0:T(8,128)(2,1)S(1)}, u32[]{:S(2)}) copy-start(bf16[4,512,128]{1,2,0:T(8,128)(2,1)S(1)} %convolution_convert_fusion.4) | copy-start | bytes 1572868
  62.6 6.0 %copy-start.16 = (f32[4,512,512]{1,2,0:T(8,128)S(1)}, f32[4,512,512]{1,2,0:T(8,128)}, u32[]{:S(2)}) copy-start(f32[4,512,512]{1,2,0:T(8,128)} %get-tuple-element.12) | copy-start | bytes 12582916
  176.6 106.6 %all-gather.7.cloned.1.call-start = ((), (), s32[]{:S(2)}) async-start(), calls=%async_computation.5 | async-start | bytes 5242880 | tf_op jit(solution)/shard_map/all_gather | solution.py:90
  222.8 2.1 copy-start.12
  222.8 2.1 copy-start.13
  228.2 4.5 %collective-permute-start = (bf16[128,4096]{1,0:T(8,128)(2,1)S(1)}, bf16[128,4096]{1,0:T(8,128)(2,1)S(1)}, u32[]{:S(2)}, u32[]{:S(2)}) collective-permute-start(bf16[128,4096]{1,0:T(8,128)(2,1)S(1)} %fusion.7), channel_id=1, source_target_pairs={{64,0},{65,1},{66,2},{67,3},{68,4},{69,5},{70,6},{71,7},{72,8},{73... | collective-permute-start | bytes 3145736 | tf_op jit(solution)/shard_map/ppermute | solution.py:118
  235.0 116.4 %reduce-scatter.6.cloned.1.call-start = ((), (), s32[]{:S(2)}) async-start(), calls=%async_computation.6 | async-start | bytes 5242880 | tf_op jit(solution)/shard_map/reduce_scatter | solution.py:97
  283.2 6.8 %copy-start.17 = (f32[4,512,512]{1,2,0:T(8,128)S(1)}, f32[4,512,512]{1,2,0:T(8,128)}, u32[]{:S(2)}) copy-start(f32[4,512,512]{1,2,0:T(8,128)} %get-tuple-element.12) | copy-start | bytes 12582916
  290.3 3.2 slice-start
  290.3 3.8 slice-start.1
  291.3 1.5 copy-start.5
  291.3 4.1 slice-start.2
  304.2 135.7 %reduce-scatter.8.cloned.1.call-start = ((), (), s32[]{:S(2)}) async-start(), calls=%async_computation.7 | async-start | bytes 8912896 | tf_op jit(solution)/shard_map/reduce_scatter | solution.py:119
  305.2 4.7 %copy-start.18 = (bf16[512,4096]{1,0:T(8,128)(2,1)S(1)}, bf16[512,4096]{1,0:T(8,128)(2,1)}, u32[]{:S(2)}) copy-start(bf16[512,4096]{1,0:T(8,128)(2,1)} %all-gather.7.cloned.1.call-done) | copy-start | bytes 12582916
  315.8 37.6 %copy-start.15 = (bf16[128,4096]{1,0:T(8,128)(2,1)S(1)}, bf16[128,4096]{1,0:T(8,128)(2,1)}, u32[]{:S(2)}) copy-start(bf16[128,4096]{1,0:T(8,128)(2,1)} %copy-done.14) | copy-start | bytes 3145732
  315.8 37.6 %copy-start.10 = (bf16[128,4096]{1,0:T(8,128)(2,1)S(1)}, bf16[128,4096]{1,0:T(8,128)(2,1)}, u32[]{:S(2)}) copy-start(bf16[128,4096]{1,0:T(8,128)(2,1)} %copy-done.9) | copy-start | bytes 3145732
  351.4 2.0 copy-start.11
  (8 other events, 8.5 us)
Sparse Core Ops, SparseCore 0:
  11.9 50.6 all-gather.4
  64.7 100.1 all-gather.8
  176.7 45.9 reduce-scatter.3
  235.2 47.9 all-gather.6
  304.3 47.1 reduce-scatter.5
  354.7 85.0 reduce-scatter.7
